TPU v7x, 32 devices: a whole 2x2x4 slice. The times are simulated.
32 devices in a mesh: gx: 4 (over x, core), gy: 8 (over z, y).
Axes of the slice: x: 2, y: 2, z: 4, core: 2. Of those that a mesh axis runs over, the one named last changes fastest.
Arguments:
- points: bfloat16 [2048, 3, 256], P(('gx', 'gy')), may hold values from 0 to 1
- charges: bfloat16 [2048, 16, 256], P(('gx', 'gy')), may hold values from -6 to 6
- near_list: int32 [2048, 8], P(('gx', 'gy')), may hold values from 0 to 2047, as said below
- near_count: int32 [2048], P(('gx', 'gy')), may hold values from 1 to 8
- far_leaf: int32 [2048, 8], P(('gx', 'gy')), may hold values from 0 to 2047, as said below
- far_cluster: int32 [256, 8], P(('gx', 'gy')), may hold values from 0 to 255, as said below
- basis: bfloat16 [2048, 64, 256], P(('gx', 'gy')), may hold values from -0.375 to 0.375
- leaf_transfer: bfloat16 [2048, 4096], P(('gx', 'gy')), may hold values from -0.5 to 0.5
- cluster_transfer: bfloat16 [256, 4096], P(('gx', 'gy')), may hold values from -0.5 to 0.5
- leaf_coupling: bfloat16 [2048, 8, 4096], P(('gx', 'gy')), may hold values from -0.25 to 0.25
- cluster_coupling: bfloat16 [256, 8, 4096], P(('gx', 'gy')), may hold values from -0.25 to 0.25
- top_transfer: bfloat16 [2, 64, 64], replicated, may hold values from -0.5 to 0.5
- top_coupling: bfloat16 [2, 64, 64], replicated, may hold values from -0.75 to 0.75
Outputs:
- potential: float32 [2048, 16, 256], P(('gx', 'gy'))
Inputs may be any that keep to these rules, and one draw needn't show every extreme that they name: `near_list`: every entry of row i is within 64 of i, and entry 0 is i itself. Slots of near_list from near_count on are not used. `far_leaf`: every entry of row i is within 64 of i. `far_cluster`: every entry of row c is within 8 of c.
All inputs are finite; a program needn't handle non-finite values.
Results may differ from a plain program's by a relative error of at most 0.0095.
Values may be sent and summed in bfloat16 or wider, within the bound.
A program may use at most 64 MiB of HBM per device.

v0:
```python
import jax
import jax.numpy as jnp
from jax import lax
from jax.sharding import PartitionSpec as P

SOFTENING = 0.0025
STRENGTH = 0.0625
ROOT_TWO = 1.4142135623730951


def extended(x, sides, width):
    for axis, dim in sides:
        devices, length = (lax.axis_size(axis), x.shape[dim])
        up = [(i, (i + 1) % devices) for i in range(devices - 1)]
        down = [(j, i) for i, j in up]
        last = lax.slice_in_dim(x, length - width, length, axis=dim)
        initial = lax.slice_in_dim(x, 0, width, axis=dim)
        before = lax.ppermute(last, axis, up)
        after = lax.ppermute(initial, axis, down)
        x = jnp.concatenate([before, x, after], axis=dim)
    return x


def partner(value, axis, distance):
    mask = 2**distance
    pairs = [(source, source ^ mask) for source in range(lax.axis_size(axis))]
    return lax.ppermute(value, axis, pairs)


def kernel_tile(target, source, live):
    squared = jnp.zeros((target.shape[0], target.shape[2], source.shape[2]), jnp.float32)
    for component in range(3):
        spread = target[:, component, :, None].astype(jnp.float32) - source[
            :, component, None, :
        ].astype(jnp.float32)
        squared = squared + spread * spread
    values = STRENGTH / jnp.sqrt(squared + SOFTENING)
    return jnp.where(live[:, None, None], values, 0.0).astype(jnp.bfloat16)


def small_product(vector, matrix):
    return jnp.dot(vector, matrix, preferred_element_type=jnp.float32)


def on_device(
    points,
    charges,
    near_list,
    near_count,
    far_leaf,
    far_cluster,
    basis,
    leaf_transfer,
    cluster_transfer,
    leaf_coupling,
    cluster_coupling,
    top_transfer,
    top_coupling,
):
    leaf_count, rhs_count, leaf_size = charges.shape
    rank_size = basis.shape[1]
    parent_count = cluster_transfer.shape[0]
    slot_count = near_list.shape[1]
    link_count = far_leaf.shape[1]
    position = lax.axis_index(("gx", "gy"))
    first_leaf = position * leaf_count
    moments = jnp.einsum("lrs,lks->lrk", charges, basis, preferred_element_type=jnp.float32).astype(
        jnp.bfloat16
    )
    wide_points, wide_charges, wide_moments = (
        extended(points, ((("gx", "gy"), 0),), leaf_count),
        extended(charges, ((("gx", "gy"), 0),), leaf_count),
        extended(moments, ((("gx", "gy"), 0),), leaf_count),
    )
    leaf_maps = leaf_transfer.reshape(leaf_count, rank_size, rank_size)
    raised = jnp.einsum("lrk,lkp->lrp", moments, leaf_maps, preferred_element_type=jnp.float32)
    parent_mom = (
        raised.reshape(parent_count, 8, rhs_count, rank_size).sum(axis=1).astype(jnp.bfloat16)
    )
    wide_parent = extended(parent_mom, ((("gx", "gy"), 0),), parent_count)
    parent_maps = cluster_transfer.reshape(parent_count, rank_size, rank_size)
    device_mom = jnp.einsum(
        "crk,ckp->rp", parent_mom, parent_maps, preferred_element_type=jnp.float32
    ).astype(jnp.bfloat16)
    level_count = lax.axis_size(("gx", "gy")).bit_length() - 1
    couplings = []
    current = device_mom
    for height in range(level_count):
        sibling = partner(current, ("gx", "gy"), height)
        on_right = position >> height & 1 == 1
        couplings.append(
            small_product(sibling, jnp.where(on_right, top_coupling[1], top_coupling[0]))
        )
        left_part = jnp.where(on_right, sibling, current)
        right_part = jnp.where(on_right, current, sibling)
        current = (
            small_product(left_part, top_transfer[0]) + small_product(right_part, top_transfer[1])
        ).astype(jnp.bfloat16)
    local_field = jnp.zeros((rhs_count, rank_size), jnp.float32)
    for height in reversed(range(level_count)):
        on_right = position >> height & 1 == 1
        down_map = jnp.where(on_right, top_transfer[1], top_transfer[0])
        local_field = couplings[height] + ROOT_TWO * small_product(
            local_field.astype(jnp.bfloat16), down_map.T
        )
    device_local = local_field.astype(jnp.bfloat16)
    near_rows = near_list - first_leaf + leaf_count

    def add_slot(slot_index, running):
        source_index = lax.dynamic_index_in_dim(near_rows, slot_index, 1, keepdims=False)
        source_points = jnp.take(wide_points, source_index, axis=0)
        source_charges = jnp.take(wide_charges, source_index, axis=0)
        tile = kernel_tile(points, source_points, slot_index < near_count)
        return running + jnp.einsum(
            "lts,lrs->lrt", tile, source_charges, preferred_element_type=jnp.float32
        )

    near_field = lax.fori_loop(
        0, slot_count, add_slot, jnp.zeros((leaf_count, rhs_count, leaf_size), jnp.float32)
    )
    parent_rows = far_cluster - position * parent_count + parent_count
    parent_coup = cluster_coupling.reshape(parent_count, link_count, rank_size, rank_size)
    parent_local = jnp.einsum(
        "cfrk,cfkp->crp",
        jnp.take(wide_parent, parent_rows, axis=0),
        parent_coup,
        preferred_element_type=jnp.float32,
    )
    parent_local = parent_local + jnp.einsum(
        "rp,ckp->crk", device_local, parent_maps, preferred_element_type=jnp.float32
    )
    parent_local = parent_local.astype(jnp.bfloat16)
    leaf_rows = far_leaf - first_leaf + leaf_count
    leaf_coup = leaf_coupling.reshape(leaf_count, link_count, rank_size, rank_size)
    leaf_local = jnp.einsum(
        "lfrk,lfkp->lrp",
        jnp.take(wide_moments, leaf_rows, axis=0),
        leaf_coup,
        preferred_element_type=jnp.float32,
    )
    leaf_local = leaf_local + jnp.einsum(
        "lrp,lkp->lrk",
        jnp.repeat(parent_local, 8, axis=0),
        leaf_maps,
        preferred_element_type=jnp.float32,
    )
    leaf_local = leaf_local.astype(jnp.bfloat16)
    return near_field + jnp.einsum(
        "lrk,lks->lrs", leaf_local, basis, preferred_element_type=jnp.float32
    )


def solution(mesh):
    in_specs = (
        P(("gx", "gy"), None, None),
        P(("gx", "gy"), None, None),
        P(("gx", "gy"), None),
        P(("gx", "gy")),
        P(("gx", "gy"), None),
        P(("gx", "gy"), None),
        P(("gx", "gy"), None, None),
        P(("gx", "gy"), None),
        P(("gx", "gy"), None),
        P(("gx", "gy"), None, None),
        P(("gx", "gy"), None, None),
        P(),
        P(),
    )
    out_specs = P(("gx", "gy"), None, None)
    return jax.shard_map(
        on_device, mesh=mesh, in_specs=in_specs, out_specs=out_specs, check_vma=False
    )
```

profile of v0, /device:TPU:2, one launch (start us, length us, event | category | flops | bytes accessed | tf_op | source)
XLA Modules:
  0.0 248.7 jit_solution(14579472692141373670)
XLA Ops:
  0.0 2.2 reshape.83
  2.2 2.1 convolution_convert_fusion
  5.3 3.4 %collective-permute-start.6 = (bf16[8,16,64]{2,1,0:T(8,128)(2,1)}, bf16[8,16,64]{2,1,0:T(8,128)(2,1)}, u32[]{:S(2)}, u32[]{:S(2)}) collective-permute-start(bf16[8,16,64]{2,1,0:T(8,128)(2,1)} %bitcast_reduce_fusion), channel_id=1, source_target_pairs={{0,1},{1,2},{2,3},{3,4},{4,5},{5,6},{6,7},{7,8},{8,9},{9,10},{10,1... | collective-permute-start | bytes 49160 | tf_op jit(solution)/shard_map/ppermute | solution.py:18
  8.8 5.7 %collective-permute-start.7 = (bf16[8,16,64]{2,1,0:T(8,128)(2,1)}, bf16[8,16,64]{2,1,0:T(8,128)(2,1)}, u32[]{:S(2)}, u32[]{:S(2)}) collective-permute-start(bf16[8,16,64]{2,1,0:T(8,128)(2,1)} %bitcast_reduce_fusion), channel_id=1, source_target_pairs={{1,0},{2,1},{3,2},{4,3},{5,4},{6,5},{7,6},{8,7},{9,8},{10,9},{11,1... | collective-permute-start | bytes 49160 | tf_op jit(solution)/shard_map/ppermute | solution.py:19
  14.5 1.9 collective-permute-start.4
  16.4 7.2 %collective-permute-start.5 = (bf16[64,16,64]{2,1,0:T(8,128)(2,1)S(1)}, bf16[64,16,64]{2,1,0:T(8,128)(2,1)}, u32[]{:S(2)}, u32[]{:S(2)}) collective-permute-start(bf16[64,16,64]{2,1,0:T(8,128)(2,1)S(1)} %convolution_convert_fusion), channel_id=1, source_target_pairs={{1,0},{2,1},{3,2},{4,3},{5,4},{6,5},{7,6},{8,7},{9,8},{10,9},{11,1... | collective-permute-start | bytes 393224 | tf_op jit(solution)/shard_map/ppermute | solution.py:19
  23.7 1.7 reshape.86
  29.2 2.4 collective-permute-done.8
  34.6 2.3 collective-permute-done.9
  41.8 1.9 collective-permute-done.10
  51.6 2.8 %reshape.85 = bf16[8,8,64,64]{3,2,1,0:T(8,128)(2,1)} reshape(bf16[8,8,4096]{2,1,0:T(8,128)(2,1)} %param.25) | data formatting | bytes 1048576 | tf_op jit(solution)/shard_map/reshape | solution.py:122
  55.8 12.6 %reshape.82 = bf16[64,8,64,64]{3,2,1,0:T(8,128)(2,1)} reshape(bf16[64,8,4096]{2,1,0:T(8,128)(2,1)} %param.24) | data formatting | bytes 8388608 | tf_op jit(solution)/shard_map/reshape | solution.py:134
  69.2 1.9 collective-permute-start.2
  75.0 7.2 %collective-permute-start.3 = (bf16[64,3,256]{2,1,0:T(4,128)(2,1)}, bf16[64,3,256]{2,1,0:T(4,128)(2,1)S(1)}, u32[]{:S(2)}, u32[]{:S(2)}) collective-permute-start(bf16[64,3,256]{2,1,0:T(4,128)(2,1)} %copy.18), channel_id=1, source_target_pairs={{1,0},{2,1},{3,2},{4,3},{5,4},{6,5},{7,6},{8,7},{9,8},{10,9},{11,1... | collective-permute-start | bytes 294920 | tf_op jit(solution)/shard_map/ppermute | solution.py:19
  82.3 1.9 collective-permute-start
  85.7 1.7 convolution_bitcast_fusion.1
  88.6 7.2 %collective-permute-start.1 = (bf16[64,16,256]{2,1,0:T(8,128)(2,1)}, bf16[64,16,256]{2,1,0:T(8,128)(2,1)}, u32[]{:S(2)}, u32[]{:S(2)}) collective-permute-start(bf16[64,16,256]{2,1,0:T(8,128)(2,1)} %param.16), channel_id=1, source_target_pairs={{1,0},{2,1},{3,2},{4,3},{5,4},{6,5},{7,6},{8,7},{9,8},{10,9},{11,1... | collective-permute-start | bytes 1572872 | tf_op jit(solution)/shard_map/ppermute | solution.py:19
  95.9 1.9 pad_maximum_fusion.2
  99.0 2.8 %gather_fusion.2 = bf16[512,16,64]{2,1,0:T(8,128)(2,1)} fusion(bf16[192,16,64]{2,1,0:T(8,128)(2,1)S(1)} %pad_maximum_fusion.1, s32[1024]{0:T(1024)S(1)} %pad_clamp_fusion.2), kind=kCustom, calls=%fused_computation.2 | custom fusion | bytes 2099200 | tf_op jit(solution)/shard_map/jit(_take)/gather | solution.py:137
  101.8 6.1 %fusion.13 = f32[64,16,64]{2,1,0:T(8,128)} fusion(bf16[64,8,64,64]{3,2,1,0:T(8,128)(2,1)} %reshape.82, bf16[64,8,16,64]{3,2,1,0:T(8,128)(2,1)} %bitcast.139, pred[64,8]{1,0:T(8,128)(4,1)} %copy.21), kind=kOutput, calls=%fused_computation.34 | convolution fusion | flops 67633152 | bytes 5505536 | tf_op jit(solution)/shard_map/lfrk,lfkp->lrp/dot_general | solution.py:135
  108.0 2.9 %fusion.17 = f32[64,16,256]{2,1,0:T(8,128)} fusion(bf16[64,64,256]{2,1,0:T(8,128)(2,1)S(1)} %copy-done, f32[64,16,64]{2,1,0:T(8,128)} %fusion.13, bf16[64,16,64]{2,1,0:T(8,128)(2,1)S(1)} %bitcast.141, bf16[64,64,64]{2,1,0:T(8,128)(2,1)S(1)} %copy-done.2), kind=kOutput, calls=%fused_computation.37 | convolution fusion | flops 42074112 | bytes 4063232 | tf_op jit(solution)/shard_map/lrk,lks->lrs/dot_general | solution.py:148
  112.5 2.7 %pad_maximum_fusion = bf16[192,16,256]{2,1,0:T(8,128)(2,1)} fusion(bf16[64,16,256]{2,1,0:T(8,128)(2,1)} %collective-permute-done.1, bf16[64,16,256]{2,1,0:T(8,128)(2,1)} %param.16, bf16[64,16,256]{2,1,0:T(8,128)(2,1)} %collective-permute-done), kind=kLoop, calls=%fused_computation.32 | loop fusion | flops 1572864 | bytes 3145728 | tf_op jit(solution)/shard_map/concatenate | solution.py:20
  115.2 130.8 %while.14 = (s32[]{:T(128)}, f32[64,16,256]{2,1,0:T(8,128)}, s32[64,8]{0,1:T(8,128)}, bf16[192,16,256]{2,1,0:T(8,128)(2,1)}, s32[64]{0:T(128)S(1)}, /*index=5*/b...) while((s32[]{:T(128)}, f32[64,16,256]{2,1,0:T(8,128)}, ...), condition=%wide.region_1.2_spmd.clone, body=%wide.region_0.0_spmd.clone.sunk | while | flops 185484736 | bytes 5445551 | solution.py:118
  115.9 1.7 gather_fusion
  117.9 2.0 gather_fusion.1
  119.9 11.0 %fusion.165 = f32[64,16,256]{2,1,0:T(8,128)} fusion(f32[64,256]{1,0:T(8,128)S(1)} %get-tuple-element.239, f32[64,256]{1,0:T(8,128)S(1)} %get-tuple-element.240, f32[64,256]{1,0:T(8,128)S(1)} %get-tuple-element.241, f32[64,256]{1,0:T(8,128)S(1)} %get-tuple-element.242, f32[64,256]{1,0:T(8,128)S(1)} %bitcast.140, ...), kind=kOutput, calls=%fused_computation.7.clone.1 | convolution fusion | flops 185335808 | bytes 3014785 | tf_op jit(solution)/shard_map/while/body/eval_jaxpr/lts,lrs->lrt/dot_general | solution.py:114
  131.7 1.7 gather_fusion
  133.7 2.0 gather_fusion.1
  135.7 11.7 %fusion.165 = f32[64,16,256]{2,1,0:T(8,128)} fusion(f32[64,256]{1,0:T(8,128)S(1)} %get-tuple-element.239, f32[64,256]{1,0:T(8,128)S(1)} %get-tuple-element.240, f32[64,256]{1,0:T(8,128)S(1)} %get-tuple-element.241, f32[64,256]{1,0:T(8,128)S(1)} %get-tuple-element.242, f32[64,256]{1,0:T(8,128)S(1)} %bitcast.140, ...), kind=kOutput, calls=%fused_computation.7.clone.1 | convolution fusion | flops 185335808 | bytes 3014785 | tf_op jit(solution)/shard_map/while/body/eval_jaxpr/lts,lrs->lrt/dot_general | solution.py:114
  148.1 1.7 gather_fusion
  150.1 2.0 gather_fusion.1
  152.2 11.7 %fusion.165 = f32[64,16,256]{2,1,0:T(8,128)} fusion(f32[64,256]{1,0:T(8,128)S(1)} %get-tuple-element.239, f32[64,256]{1,0:T(8,128)S(1)} %get-tuple-element.240, f32[64,256]{1,0:T(8,128)S(1)} %get-tuple-element.241, f32[64,256]{1,0:T(8,128)S(1)} %get-tuple-element.242, f32[64,256]{1,0:T(8,128)S(1)} %bitcast.140, ...), kind=kOutput, calls=%fused_computation.7.clone.1 | convolution fusion | flops 185335808 | bytes 3014785 | tf_op jit(solution)/shard_map/while/body/eval_jaxpr/lts,lrs->lrt/dot_general | solution.py:114
  164.5 1.7 gather_fusion
  166.6 2.0 gather_fusion.1
  168.6 11.7 %fusion.165 = f32[64,16,256]{2,1,0:T(8,128)} fusion(f32[64,256]{1,0:T(8,128)S(1)} %get-tuple-element.239, f32[64,256]{1,0:T(8,128)S(1)} %get-tuple-element.240, f32[64,256]{1,0:T(8,128)S(1)} %get-tuple-element.241, f32[64,256]{1,0:T(8,128)S(1)} %get-tuple-element.242, f32[64,256]{1,0:T(8,128)S(1)} %bitcast.140, ...), kind=kOutput, calls=%fused_computation.7.clone.1 | convolution fusion | flops 185335808 | bytes 3014785 | tf_op jit(solution)/shard_map/while/body/eval_jaxpr/lts,lrs->lrt/dot_general | solution.py:114
  181.0 1.7 gather_fusion
  183.0 2.0 gather_fusion.1
  185.0 11.7 %fusion.165 = f32[64,16,256]{2,1,0:T(8,128)} fusion(f32[64,256]{1,0:T(8,128)S(1)} %get-tuple-element.239, f32[64,256]{1,0:T(8,128)S(1)} %get-tuple-element.240, f32[64,256]{1,0:T(8,128)S(1)} %get-tuple-element.241, f32[64,256]{1,0:T(8,128)S(1)} %get-tuple-element.242, f32[64,256]{1,0:T(8,128)S(1)} %bitcast.140, ...), kind=kOutput, calls=%fused_computation.7.clone.1 | convolution fusion | flops 185335808 | bytes 3014785 | tf_op jit(solution)/shard_map/while/body/eval_jaxpr/lts,lrs->lrt/dot_general | solution.py:114
  197.4 1.7 gather_fusion
  199.4 2.0 gather_fusion.1
  201.5 11.7 %fusion.165 = f32[64,16,256]{2,1,0:T(8,128)} fusion(f32[64,256]{1,0:T(8,128)S(1)} %get-tuple-element.239, f32[64,256]{1,0:T(8,128)S(1)} %get-tuple-element.240, f32[64,256]{1,0:T(8,128)S(1)} %get-tuple-element.241, f32[64,256]{1,0:T(8,128)S(1)} %get-tuple-element.242, f32[64,256]{1,0:T(8,128)S(1)} %bitcast.140, ...), kind=kOutput, calls=%fused_computation.7.clone.1 | convolution fusion | flops 185335808 | bytes 3014785 | tf_op jit(solution)/shard_map/while/body/eval_jaxpr/lts,lrs->lrt/dot_general | solution.py:114
  213.8 1.7 gather_fusion
  215.9 2.0 gather_fusion.1
  217.9 11.7 %fusion.165 = f32[64,16,256]{2,1,0:T(8,128)} fusion(f32[64,256]{1,0:T(8,128)S(1)} %get-tuple-element.239, f32[64,256]{1,0:T(8,128)S(1)} %get-tuple-element.240, f32[64,256]{1,0:T(8,128)S(1)} %get-tuple-element.241, f32[64,256]{1,0:T(8,128)S(1)} %get-tuple-element.242, f32[64,256]{1,0:T(8,128)S(1)} %bitcast.140, ...), kind=kOutput, calls=%fused_computation.7.clone.1 | convolution fusion | flops 185335808 | bytes 3014785 | tf_op jit(solution)/shard_map/while/body/eval_jaxpr/lts,lrs->lrt/dot_general | solution.py:114
  230.3 1.7 gather_fusion
  232.3 2.0 gather_fusion.1
  234.3 11.7 %fusion.165 = f32[64,16,256]{2,1,0:T(8,128)} fusion(f32[64,256]{1,0:T(8,128)S(1)} %get-tuple-element.239, f32[64,256]{1,0:T(8,128)S(1)} %get-tuple-element.240, f32[64,256]{1,0:T(8,128)S(1)} %get-tuple-element.241, f32[64,256]{1,0:T(8,128)S(1)} %get-tuple-element.242, f32[64,256]{1,0:T(8,128)S(1)} %bitcast.140, ...), kind=kOutput, calls=%fused_computation.7.clone.1 | convolution fusion | flops 185335808 | bytes 3014785 | tf_op jit(solution)/shard_map/while/body/eval_jaxpr/lts,lrs->lrt/dot_general | solution.py:114
  246.0 2.7 %add.163 = f32[64,16,256]{2,1,0:T(8,128)} add(f32[64,16,256]{2,1,0:T(8,128)} %get-tuple-element.129, f32[64,16,256]{2,1,0:T(8,128)} %fusion.17) | non-fusion elementwise | flops 262144 | bytes 3145728 | tf_op jit(solution)/shard_map/add | solution.py:148
  (128 shorter events, 40.3 us)
Async XLA Ops:
  0.0 2.2 copy-start
  2.2 66.2 %copy-start.1 = (bf16[64,64,64]{2,1,0:T(8,128)(2,1)}, bf16[64,64,64]{2,1,0:T(8,128)(2,1)S(1)}, u32[]{:S(2)}) copy-start(bf16[64,64,64]{2,1,0:T(8,128)(2,1)S(1)} %reshape.83) | copy-start | bytes 1572868
  4.3 64.2 %copy-start.3 = (bf16[64,3,256]{2,0,1:T(8,128)(2,1)S(1)}, bf16[64,3,256]{2,0,1:T(8,128)(2,1)}, u32[]{:S(2)}) copy-start(bf16[64,3,256]{2,0,1:T(8,128)(2,1)} %param.15) | copy-start | bytes 294916
  4.3 66.8 %copy-start.4 = (bf16[2,64,64]{2,1,0:T(8,128)(2,1)S(1)}, bf16[2,64,64]{2,1,0:T(8,128)(2,1)}, u32[]{:S(2)}) copy-start(bf16[2,64,64]{2,1,0:T(8,128)(2,1)} %param.26) | copy-start | bytes 49156
  5.3 69.7 %collective-permute-start.6 = (bf16[8,16,64]{2,1,0:T(8,128)(2,1)}, bf16[8,16,64]{2,1,0:T(8,128)(2,1)}, u32[]{:S(2)}, u32[]{:S(2)}) collective-permute-start(bf16[8,16,64]{2,1,0:T(8,128)(2,1)} %bitcast_reduce_fusion), channel_id=1, source_target_pairs={{0,1},{1,2},{2,3},{3,4},{4,5},{5,6},{6,7},{7,8},{8,9},{9,10},{10,1... | collective-permute-start | bytes 49160 | tf_op jit(solution)/shard_map/ppermute | solution.py:18
  8.8 73.5 %collective-permute-start.7 = (bf16[8,16,64]{2,1,0:T(8,128)(2,1)}, bf16[8,16,64]{2,1,0:T(8,128)(2,1)}, u32[]{:S(2)}, u32[]{:S(2)}) collective-permute-start(bf16[8,16,64]{2,1,0:T(8,128)(2,1)} %bitcast_reduce_fusion), channel_id=1, source_target_pairs={{1,0},{2,1},{3,2},{4,3},{5,4},{6,5},{7,6},{8,7},{9,8},{10,9},{11,1... | collective-permute-start | bytes 49160 | tf_op jit(solution)/shard_map/ppermute | solution.py:19
  14.5 83.3 %collective-permute-start.4 = (bf16[64,16,64]{2,1,0:T(8,128)(2,1)S(1)}, bf16[64,16,64]{2,1,0:T(8,128)(2,1)}, u32[]{:S(2)}, u32[]{:S(2)}) collective-permute-start(bf16[64,16,64]{2,1,0:T(8,128)(2,1)S(1)} %convolution_convert_fusion), channel_id=1, source_target_pairs={{0,1},{1,2},{2,3},{3,4},{4,5},{5,6},{6,7},{7,8},{8,9},{9,10},{10,1... | collective-permute-start | bytes 393224 | tf_op jit(solution)/shard_map/ppermute | solution.py:18
  16.4 81.4 %collective-permute-start.5 = (bf16[64,16,64]{2,1,0:T(8,128)(2,1)S(1)}, bf16[64,16,64]{2,1,0:T(8,128)(2,1)}, u32[]{:S(2)}, u32[]{:S(2)}) collective-permute-start(bf16[64,16,64]{2,1,0:T(8,128)(2,1)S(1)} %convolution_convert_fusion), channel_id=1, source_target_pairs={{1,0},{2,1},{3,2},{4,3},{5,4},{6,5},{7,6},{8,7},{9,8},{10,9},{11,1... | collective-permute-start | bytes 393224 | tf_op jit(solution)/shard_map/ppermute | solution.py:19
  26.5 5.2 %collective-permute-start.8 = (bf16[16,64]{1,0:T(8,128)(2,1)S(1)}, bf16[16,64]{1,0:T(8,128)(2,1)S(1)}, u32[]{:S(2)}, u32[]{:S(2)}) collective-permute-start(bf16[16,64]{1,0:T(8,128)(2,1)S(1)} %fusion.20), channel_id=1, source_target_pairs={{0,1},{1,0},{2,3},{3,2},{4,5},{5,4},{6,7},{7,6},{8,9},{9,8},{10,11... | collective-permute-start | bytes 6152 | tf_op jit(solution)/shard_map/ppermute | solution.py:27
  33.3 3.6 %collective-permute-start.9 = (bf16[16,64]{1,0:T(8,128)(2,1)S(1)}, bf16[16,64]{1,0:T(8,128)(2,1)S(1)}, u32[]{:S(2)}, u32[]{:S(2)}) collective-permute-start(bf16[16,64]{1,0:T(8,128)(2,1)S(1)} %fusion.22), channel_id=1, source_target_pairs={{0,2},{1,3},{2,0},{3,1},{4,6},{5,7},{6,4},{7,5},{8,10},{9,11},{10,... | collective-permute-start | bytes 6152 | tf_op jit(solution)/shard_map/ppermute | solution.py:27
  36.9 0.6 copy-start.5
  39.2 4.5 %collective-permute-start.10 = (bf16[16,64]{1,0:T(8,128)(2,1)S(1)}, bf16[16,64]{1,0:T(8,128)(2,1)S(1)}, u32[]{:S(2)}, u32[]{:S(2)}) collective-permute-start(bf16[16,64]{1,0:T(8,128)(2,1)S(1)} %fusion.24), channel_id=1, source_target_pairs={{0,4},{1,5},{2,6},{3,7},{4,0},{5,1},{6,2},{7,3},{8,12},{9,13},{10,... | collective-permute-start | bytes 6152 | tf_op jit(solution)/shard_map/ppermute | solution.py:27
  43.7 0.6 copy-start.7
  46.0 2.7 %collective-permute-start.11 = (bf16[16,64]{1,0:T(8,128)(2,1)S(1)}, bf16[16,64]{1,0:T(8,128)(2,1)}, u32[]{:S(2)}, u32[]{:S(2)}) collective-permute-start(bf16[16,64]{1,0:T(8,128)(2,1)S(1)} %fusion.26), channel_id=1, source_target_pairs={{0,8},{1,9},{2,10},{3,11},{4,12},{5,13},{6,14},{7,15},{8,0},{9,1},... | collective-permute-start | bytes 6152 | tf_op jit(solution)/shard_map/ppermute | solution.py:27
  47.3 26.7 %copy-start.6 = (bf16[16,64]{1,0:T(8,128)(2,1)S(1)}, bf16[16,64]{1,0:T(8,128)(2,1)}, u32[]{:S(2)}) copy-start(bf16[16,64]{1,0:T(8,128)(2,1)} %copy-done.5) | copy-start | bytes 6148
  51.0 18.2 %collective-permute-start.12 = (bf16[16,64]{1,0:T(8,128)(2,1)}, bf16[16,64]{1,0:T(8,128)(2,1)}, u32[]{:S(2)}, u32[]{:S(2)}) collective-permute-start(bf16[16,64]{1,0:T(8,128)(2,1)} %fusion.28), channel_id=1, source_target_pairs={{0,16},{1,17},{2,18},{3,19},{4,20},{5,21},{6,22},{7,23},{8,24},{9,... | collective-permute-start | bytes 6152 | tf_op jit(solution)/shard_map/ppermute | solution.py:27
  69.2 19.4 %collective-permute-start.2 = (bf16[64,3,256]{2,1,0:T(4,128)(2,1)}, bf16[64,3,256]{2,1,0:T(4,128)(2,1)S(1)}, u32[]{:S(2)}, u32[]{:S(2)}) collective-permute-start(bf16[64,3,256]{2,1,0:T(4,128)(2,1)} %copy.18), channel_id=1, source_target_pairs={{0,1},{1,2},{2,3},{3,4},{4,5},{5,6},{6,7},{7,8},{8,9},{9,10},{10,1... | collective-permute-start | bytes 294920 | tf_op jit(solution)/shard_map/ppermute | solution.py:18
  75.0 20.8 %collective-permute-start.3 = (bf16[64,3,256]{2,1,0:T(4,128)(2,1)}, bf16[64,3,256]{2,1,0:T(4,128)(2,1)S(1)}, u32[]{:S(2)}, u32[]{:S(2)}) collective-permute-start(bf16[64,3,256]{2,1,0:T(4,128)(2,1)} %copy.18), channel_id=1, source_target_pairs={{1,0},{2,1},{3,2},{4,3},{5,4},{6,5},{7,6},{8,7},{9,8},{10,9},{11,1... | collective-permute-start | bytes 294920 | tf_op jit(solution)/shard_map/ppermute | solution.py:19
  82.3 28.6 %collective-permute-start = (bf16[64,16,256]{2,1,0:T(8,128)(2,1)}, bf16[64,16,256]{2,1,0:T(8,128)(2,1)}, u32[]{:S(2)}, u32[]{:S(2)}) collective-permute-start(bf16[64,16,256]{2,1,0:T(8,128)(2,1)} %param.16), channel_id=1, source_target_pairs={{0,1},{1,2},{2,3},{3,4},{4,5},{5,6},{6,7},{7,8},{8,9},{9,10},{10,1... | collective-permute-start | bytes 1572872 | tf_op jit(solution)/shard_map/ppermute | solution.py:18
  88.6 23.9 %collective-permute-start.1 = (bf16[64,16,256]{2,1,0:T(8,128)(2,1)}, bf16[64,16,256]{2,1,0:T(8,128)(2,1)}, u32[]{:S(2)}, u32[]{:S(2)}) collective-permute-start(bf16[64,16,256]{2,1,0:T(8,128)(2,1)} %param.16), channel_id=1, source_target_pairs={{1,0},{2,1},{3,2},{4,3},{5,4},{6,5},{7,6},{8,7},{9,8},{10,9},{11,1... | collective-permute-start | bytes 1572872 | tf_op jit(solution)/shard_map/ppermute | solution.py:19
  101.8 6.2 %copy-start.2 = (bf16[64,64,64]{2,1,0:T(8,128)(2,1)S(1)}, bf16[64,64,64]{2,1,0:T(8,128)(2,1)}, u32[]{:S(2)}) copy-start(bf16[64,64,64]{2,1,0:T(8,128)(2,1)} %copy-done.1) | copy-start | bytes 1572868
  107.9 7.2 %copy-start.8 = (s32[64]{0:T(128)S(1)}, s32[64]{0:T(128)}, u32[]{:S(2)}) copy-start(s32[64]{0:T(128)} %param.18) | copy-start | bytes 772
where the time goes:
time: 252 us; the launch traced here: 249 us
  matrix products  121 us (48%)
  local copies, waits for them, and re-layouts  59.2 us (23%)
  starting transfers between devices  36.6 us (15%)
  other arithmetic  22.5 us (9%)
  waiting for transfers between devices  8.2 us (3%)
    dot_general x8, matrix products, add_slot(): jnp.einsum('lts,lrs->lrt', tile, source_charges, preferred_element_type=j...  92.6 us
    ppermute x4, starting transfers between devices, extended(): after = lax.ppermute(initial, axis, down)  27.4 us
    gather x8, local copies, waits for them, and re-layouts, add_slot(): source_charges = jnp.take(wide_charges, source_index, axis=0)  16 us
    gather x8, local copies, waits for them, and re-layouts, add_slot(): source_points = jnp.take(wide_points, source_index, axis=0)  13.5 us
    dot_general x13, matrix products, small_product(): return jnp.dot(vector, matrix, preferred_element_type=jnp.float32)  12.7 us
    reshape x1, local copies, waits for them, and re-layouts, on_device(): leaf_coupling.reshape(leaf_count, link_count, rank_size, rank_size)  12.6 us
    ppermute x4, starting transfers between devices, extended(): before = lax.ppermute(last, axis, up)  9.17 us
    concatenate x4, other arithmetic, extended(): x = jnp.concatenate([before, x, after], axis=dim)  6.66 us
  transfers between devices with their start and end apart: 13, of which 4 were waited for; matrix products, arithmetic and copies ran while one was open for 25% of the time, Pallas kernels for 0%

commit v1 on v0

v1 whole, which is shorter than its diff:
```python
import functools

import jax
import jax.numpy as jnp
from jax import lax
from jax.experimental import pallas as pl
from jax.experimental.pallas import tpu as pltpu
from jax.sharding import PartitionSpec as P

SOFTENING = 0.0025
ROOT_TWO = 1.4142135623730951
MESH = pl.DeviceIdType.MESH
F32 = jnp.float32
BF16 = jnp.bfloat16
ROWS = 16


def dot(a, b, left=1, right=0):
    return lax.dot_general(a, b, (((left,), (right,)), ((), ())), preferred_element_type=F32)


def spread_map(parity, rank, links):
    lane = lax.broadcasted_iota(jnp.int32, (rank, rank // 2 * links), 1)
    row = lax.broadcasted_iota(jnp.int32, (rank, rank // 2 * links), 0)
    return jnp.where(row == lane // links * 2 + parity, 1.0, 0.0).astype(BF16)


def link_mask(rows, links, lanes, per_link):
    lane = lax.broadcasted_iota(jnp.int32, (rows, lanes), 1)
    row = lax.broadcasted_iota(jnp.int32, (rows, lanes), 0)
    return jnp.where(lane % links == row // per_link, 1.0, 0.0)


def fold(product, rhs, rank):
    return product[:rhs, :rank] + product[rhs:, rank:]


def gathered_up(stack, maps, mask, links, rhs):
    halves = []
    for spread in maps:
        wide = dot(stack, spread) * mask
        halves.append(wide.reshape(links, rhs, wide.shape[1]).sum(axis=0))
    return jnp.concatenate(halves, axis=0).astype(BF16)


def block_diagonal(value):
    zero = jnp.zeros_like(value)
    upper = jnp.concatenate([value, zero], axis=1)
    lower = jnp.concatenate([zero, value], axis=1)
    return jnp.concatenate([upper, lower], axis=0).astype(BF16)


def spread_down(value, matrix, maps, mask, links, rhs):
    product = dot(block_diagonal(value), matrix, 1, 1)
    total = None
    for parity, spread in enumerate(maps):
        half = product[parity * rhs : (parity + 1) * rhs]
        tall = (jnp.concatenate([half] * links, axis=0) * mask).astype(BF16)
        part = dot(tall, spread, 1, 1)
        total = part if total is None else total + part
    return total


def exchange_kernel(
    grid_shape,
    points,
    charges,
    basis,
    leaf_maps,
    parent_maps,
    top_transfer,
    top_coupling,
    wide_points,
    wide_charges,
    wide_moments,
    wide_parents,
    device_local,
    sent,
    arrived,
    send_sem,
    recv_sem,
    tree_send,
    tree_recv,
    own_sem,
):
    across, along = grid_shape
    total = across * along
    levels = total.bit_length() - 1
    me = lax.axis_index("gx") * along + lax.axis_index("gy")
    leaves, rhs, _ = charges.shape
    rank = basis.shape[1]
    parents = leaf_maps.shape[0]
    links = leaves // parents

    def place(index):
        return (index // along, index % along)

    def sibling(height):
        step = 2**height
        return me + step - 2 * step * ((me // step) % 2)

    barrier = pltpu.get_barrier_semaphore()

    @pl.when(me > 0)
    def _():
        pl.semaphore_signal(barrier, inc=1, device_id=place(me - 1), device_id_type=MESH)

    @pl.when(me < total - 1)
    def _():
        pl.semaphore_signal(barrier, inc=1, device_id=place(me + 1), device_id_type=MESH)

    for height in range(levels):
        pl.semaphore_signal(barrier, inc=1, device_id=place(sibling(height)), device_id_type=MESH)

    own_points = pltpu.make_async_copy(points, wide_points.at[1], own_sem.at[0])
    own_charges = pltpu.make_async_copy(charges, wide_charges.at[1], own_sem.at[1])
    own_points.start()
    own_charges.start()

    group = 4

    def one_moment(step, carry):
        for inner in range(group):
            leaf = step * group + inner
            value = dot(charges[leaf], basis[leaf], 1, 1).astype(BF16)
            wide_moments[1, pl.ds(pl.multiple_of(leaf * rhs, rhs), rhs), :] = value
        return carry

    lax.fori_loop(0, leaves // group, one_moment, 0)
    maps = [spread_map(parity, rank, links) for parity in range(2)]
    mask = link_mask(links * rhs, links, rank // 2 * links, rhs)
    for parent in range(parents):
        stack = wide_moments[1, parent * links * rhs : (parent + 1) * links * rhs, :]
        product = dot(gathered_up(stack, maps, mask, links, rhs), leaf_maps[parent])
        wide_parents[1, parent * rhs : (parent + 1) * rhs, :] = fold(product, rhs, rank).astype(BF16)
    product = dot(gathered_up(wide_parents[1], maps, mask, parents, rhs), parent_maps[...])
    current = fold(product, rhs, rank).astype(BF16)
    sent[0] = current

    pl.semaphore_wait(barrier, levels + jnp.where(me > 0, 1, 0) + jnp.where(me < total - 1, 1, 0))

    sources = (
        (wide_parents.at[1], wide_parents),
        (wide_moments.at[1], wide_moments),
        (points, wide_points),
        (charges, wide_charges),
    )

    def rightward(index):
        source, target = sources[index]
        return pltpu.make_async_remote_copy(
            src_ref=source,
            dst_ref=target.at[0],
            send_sem=send_sem.at[index, 0],
            recv_sem=recv_sem.at[index, 0],
            device_id=place(jnp.minimum(me + 1, total - 1)),
            device_id_type=MESH,
        )

    def leftward(index):
        source, target = sources[index]
        return pltpu.make_async_remote_copy(
            src_ref=source,
            dst_ref=target.at[2],
            send_sem=send_sem.at[index, 1],
            recv_sem=recv_sem.at[index, 1],
            device_id=place(jnp.maximum(me - 1, 0)),
            device_id_type=MESH,
        )

    def climb(height):
        return pltpu.make_async_remote_copy(
            src_ref=sent.at[height],
            dst_ref=arrived.at[height],
            send_sem=tree_send.at[height],
            recv_sem=tree_recv.at[height],
            device_id=place(sibling(height)),
            device_id_type=MESH,
        )

    climb(0).start()

    @pl.when(me < total - 1)
    def _():
        for index in range(len(sources)):
            rightward(index).start()

    @pl.when(me > 0)
    def _():
        for index in range(len(sources)):
            leftward(index).start()

    couplings = []
    sides = []
    for height in range(levels):
        climb(height).wait()
        side = (me // 2**height) % 2
        sides.append(side)
        other = arrived[height]
        couplings.append(dot(other, top_coupling[side]))
        if height < levels - 1:
            raised = dot(sent[height], top_transfer[side]) + dot(other, top_transfer[1 - side])
            sent[height + 1] = raised.astype(BF16)
            climb(height + 1).start()
    field = couplings[levels - 1]
    for height in reversed(range(levels - 1)):
        field = couplings[height] + ROOT_TWO * dot(field.astype(BF16), top_transfer[sides[height]], 1, 1)
    device_local[...] = field.astype(BF16)

    own_points.wait()
    own_charges.wait()

    @pl.when(me < total - 1)
    def _():
        for index in range(len(sources)):
            rightward(index).wait_send()
            leftward(index).wait_recv()

    @pl.when(me > 0)
    def _():
        for index in range(len(sources)):
            leftward(index).wait_send()
            rightward(index).wait_recv()


def local_kernel(
    grid_shape,
    near_list,
    near_count,
    far_leaf,
    far_cluster,
    points,
    charges,
    moments,
    parent_moments,
    device_local,
    leaf_maps,
    parent_maps,
    parent_couplings,
    leaf_couplings_hbm,
    basis_hbm,
    potential,
    leaf_couplings,
    basis,
    target_table,
    source_table,
    moment_table,
    parent_table,
    near,
    far,
    local,
    pair_source,
    pair_target,
    sems,
):
    along = grid_shape[1]
    me = lax.axis_index("gx") * along + lax.axis_index("gy")
    _, leaves, rhs, size = charges.shape
    wide = 3 * leaves
    rank = basis.shape[1]
    parents = leaf_maps.shape[0]
    links = leaves // parents
    slots = near_list.shape[0] // leaves
    get_coupling = pltpu.make_async_copy(leaf_couplings_hbm, leaf_couplings, sems.at[0])
    get_basis = pltpu.make_async_copy(basis_hbm, basis, sems.at[1])
    get_coupling.start()
    get_basis.start()

    shift = leaves - me * leaves

    def list_leaf(leaf, count):
        used = near_count[leaf]
        for slot in range(slots):
            pair_source[count] = near_list[leaf * slots + slot] + shift
            pair_target[count] = leaf
            count = count + jnp.where(slot < used, 1, 0)
        return count

    pairs = lax.fori_loop(0, leaves, list_leaf, 0)
    group = 4
    for extra in range(group):
        pair_source[pairs + extra] = leaves
        pair_target[pairs + extra] = leaves

    zero = jnp.zeros((16, size), F32)
    one = jnp.ones((16, size), F32)
    for block in range(3):
        for start in range(0, leaves, 16):
            at = block * leaves + start
            own = [points[block, axis, start : start + 16, :].astype(F32) for axis in range(3)]
            norm = own[0] * own[0] + own[1] * own[1] + own[2] * own[2]

            def split(value):
                first = value.astype(BF16).astype(F32)
                second = (value - first).astype(BF16).astype(F32)
                return [first, second, value - first - second]

            source_rows = [-512.0 * value for value in own]
            source_rows += [256.0 * value for value in split(norm + SOFTENING)] + [256.0 * one] * 3
            target_rows = own + [one] * 3 + split(norm)
            for row in range(ROWS):
                value = source_rows[row] if row < 9 else zero
                for half in range(size // 128):
                    base = (half * ROWS + row) * wide + at
                    source_table[base : base + 16, :] = value[:, half * 128 : half * 128 + 128]
                if block == 1:
                    value = target_rows[row] if row < 9 else zero
                    for half in range(size // 128):
                        base = (half * ROWS + row) * leaves + start
                        target_table[base : base + 16, :] = value[:, half * 128 : half * 128 + 128]
    near[...] = jnp.zeros_like(near)

    def side_of(table, leaf, stride):
        pieces = [
            table[pl.ds(half * ROWS * stride + leaf, ROWS, stride=stride), :]
            for half in range(size // 128)
        ]
        return jnp.concatenate(pieces, axis=1).astype(BF16)

    def some_pairs(step, carry):
        results = []
        for inner in range(group):
            source = pair_source[step * group + inner]
            target = pair_target[step * group + inner]
            source_side = side_of(source_table, source, wide)
            safe = jnp.minimum(target, leaves - 1)
            target_side = side_of(target_table, safe, leaves)
            squared = dot(source_side, target_side, 0, 0)
            tile = lax.rsqrt(squared).astype(BF16)
            results.append((target, dot(charges[source // leaves, source % leaves], tile)))
        for target, value in results:
            near[target] = near[target] + value
        return carry

    lax.fori_loop(0, (pairs + group - 1) // group, some_pairs, 0)

    maps = [spread_map(parity, rank, links) for parity in range(2)]
    for block in range(3):
        for parity in range(2):
            value = dot(moments[block], maps[parity]).astype(BF16)
            moment_table[
                block * leaves : (block + 1) * leaves, parity * rhs : (parity + 1) * rhs, :
            ] = value.reshape(leaves, rhs, value.shape[1])
            value = dot(parent_moments[block], maps[parity]).astype(BF16)
            parent_table[
                block * parents : (block + 1) * parents, parity * rhs : (parity + 1) * rhs, :
            ] = value.reshape(parents, rhs, value.shape[1])
    lanes = rank // 2 * links
    lane = lax.broadcasted_iota(jnp.int32, (2 * rhs, lanes), 1) % links
    masks = [jnp.where(lane == link, 1.0, 0.0).astype(BF16) for link in range(links)]

    def collect(table, index, row, offset):
        total = None
        for link in range(links):
            part = table[index[row * links + link] + offset] * masks[link]
            total = part if total is None else total + part
        return total

    parent_shift = parents - me * parents
    mask = link_mask(links * rhs, links, lanes, rhs)
    down = spread_down(device_local[...].astype(F32), parent_maps[...], maps, mask, links, rhs)
    parent_local = []
    for parent in range(parents):
        product = dot(collect(parent_table, far_cluster, parent, parent_shift), parent_couplings[parent])
        value = fold(product, rhs, rank) + down[parent * rhs : (parent + 1) * rhs]
        parent_local.append(value.astype(BF16).astype(F32))
    get_coupling.wait()

    def some_leaves(step, carry):
        for inner in range(group):
            leaf = step * group + inner
            product = dot(collect(moment_table, far_leaf, leaf, shift), leaf_couplings[leaf])
            far[pl.ds(pl.multiple_of(leaf * rhs, rhs), rhs), :] = fold(product, rhs, rank)
        return carry

    lax.fori_loop(0, leaves // group, some_leaves, 0)
    for parent in range(parents):
        down = spread_down(parent_local[parent], leaf_maps[parent], maps, mask, links, rhs)
        rows = slice(parent * links * rhs, (parent + 1) * links * rhs)
        local[rows, :] = (far[rows, :] + down).astype(BF16)
    get_basis.wait()

    def finish(step, carry):
        for inner in range(group):
            leaf = step * group + inner
            value = local[pl.ds(pl.multiple_of(leaf * rhs, rhs), rhs), :]
            potential[leaf] = near[leaf] + dot(value, basis[leaf])
        return carry

    lax.fori_loop(0, leaves // group, finish, 0)


def stored(matrix, links):
    length = matrix.shape[-1]
    tiles = length // 128
    value = matrix.reshape(-1, links, tiles, 128).transpose(0, 2, 1, 3)
    return value.reshape(-1, tiles * links, 128)


def on_device(
    grid_shape,
    points,
    charges,
    near_list,
    near_count,
    far_leaf,
    far_cluster,
    basis,
    leaf_transfer,
    cluster_transfer,
    leaf_coupling,
    cluster_coupling,
    top_transfer,
    top_coupling,
):
    leaves, rhs, size = charges.shape
    rank = basis.shape[1]
    parents = cluster_transfer.shape[0]
    links = far_leaf.shape[1]
    levels = (grid_shape[0] * grid_shape[1]).bit_length() - 1
    turned = points.transpose(1, 0, 2)
    leaf_maps = stored(leaf_transfer, links)
    parent_maps = stored(cluster_transfer, links)[0]
    leaf_couplings = stored(leaf_coupling, links)
    parent_couplings = stored(cluster_coupling, links)
    vmem = pl.BlockSpec(memory_space=pltpu.VMEM)
    smem = pl.BlockSpec(memory_space=pltpu.SMEM)
    hbm = pl.BlockSpec(memory_space=pl.ANY)
    shape = jax.ShapeDtypeStruct
    wide_points, wide_charges, moments, parent_moments, device_local = pl.pallas_call(
        functools.partial(exchange_kernel, grid_shape),
        out_shape=(
            shape((3,) + turned.shape, BF16),
            shape((3,) + charges.shape, BF16),
            shape((3, leaves * rhs, rank), BF16),
            shape((3, parents * rhs, rank), BF16),
            shape((rhs, rank), BF16),
        ),
        in_specs=[vmem] * 7,
        out_specs=(hbm, hbm, vmem, vmem, vmem),
        scratch_shapes=[
            pltpu.VMEM((levels, rhs, rank), BF16),
            pltpu.VMEM((levels, rhs, rank), BF16),
            pltpu.SemaphoreType.DMA((4, 2)),
            pltpu.SemaphoreType.DMA((4, 2)),
            pltpu.SemaphoreType.DMA((levels,)),
            pltpu.SemaphoreType.DMA((levels,)),
            pltpu.SemaphoreType.DMA((2,)),
        ],
        compiler_params=pltpu.CompilerParams(
            collective_id=0, has_side_effects=True, vmem_limit_bytes=32 << 20
        ),
        name="exchange",
    )(turned, charges, basis, leaf_maps, parent_maps, top_transfer, top_coupling)
    slots = near_list.shape[1]
    return pl.pallas_call(
        functools.partial(local_kernel, grid_shape),
        out_shape=shape((leaves, rhs, size), F32),
        in_specs=[smem] * 4 + [vmem] * 8 + [hbm] * 2,
        out_specs=vmem,
        scratch_shapes=[
            pltpu.VMEM(leaf_couplings.shape, BF16),
            pltpu.VMEM(basis.shape, BF16),
            pltpu.VMEM((size // 128 * ROWS * leaves, 128), F32),
            pltpu.VMEM((size // 128 * ROWS * 3 * leaves, 128), F32),
            pltpu.VMEM((3 * leaves, 2 * rhs, rank // 2 * links), BF16),
            pltpu.VMEM((3 * parents, 2 * rhs, rank // 2 * links), BF16),
            pltpu.VMEM((leaves + 1, rhs, size), F32),
            pltpu.VMEM((leaves * rhs, rank), F32),
            pltpu.VMEM((leaves * rhs, rank), BF16),
            pltpu.SMEM((leaves * slots + 8,), jnp.int32),
            pltpu.SMEM((leaves * slots + 8,), jnp.int32),
            pltpu.SemaphoreType.DMA((2,)),
        ],
        compiler_params=pltpu.CompilerParams(vmem_limit_bytes=48 << 20),
        name="local",
    )(
        near_list.reshape(-1),
        near_count,
        far_leaf.reshape(-1),
        far_cluster.reshape(-1),
        wide_points,
        wide_charges,
        moments,
        parent_moments,
        device_local,
        leaf_maps,
        parent_maps,
        parent_couplings,
        leaf_couplings,
        basis,
    )


def solution(mesh):
    grid_shape = (mesh.shape["gx"], mesh.shape["gy"])
    both = ("gx", "gy")
    in_specs = (
        P(both, None, None),
        P(both, None, None),
        P(both, None),
        P(both),
        P(both, None),
        P(both, None),
        P(both, None, None),
        P(both, None),
        P(both, None),
        P(both, None, None),
        P(both, None, None),
        P(),
        P(),
    )
    return jax.shard_map(
        functools.partial(on_device, grid_shape),
        mesh=mesh,
        in_specs=in_specs,
        out_specs=P(both, None, None),
        check_vma=False,
    )
```

time: 252 us -> 148 us (0.59)
  the two profiles are of different devices: /device:TPU:2 before, /device:TPU:25 now
where the time goes in v1:
time: 148 us
  Pallas kernels  138 us (93%)
  local copies, waits for them, and re-layouts  9.45 us (6%)
    pallas_call x1, Pallas kernels, on_device(): pl.pallas_call(functools.partial(local_kernel, grid_shape), out_shape=sha...  92 us
    pallas_call x1, Pallas kernels, on_device(): pl.pallas_call(functools.partial(exchange_kernel, grid_shape), out_shape=...  46.4 us
    unnamed x26, local copies, waits for them, and re-layouts  8.48 us

profile of v1, /device:TPU:25, one launch (start us, length us, event | category | flops | bytes accessed | tf_op | source)
XLA Modules:
  0.0 147.9 jit_solution(2240028524470046093)
XLA Ops:
  0.0 0.0 copy-start.7
  0.0 0.0 copy-start.11
  0.0 0.8 reshape.32.far_cluster
  0.8 0.8 copy.14
  1.6 0.1 reshape.30.near_list
  1.7 0.8 copy.15
  2.4 0.1 reshape.31.far_leaf
  2.5 0.0 copy-start
  2.5 1.6 %copy-done = bf16[64,64,256]{2,1,0:T(8,128)(2,1)S(1)} copy-done((bf16[64,64,256]{2,1,0:T(8,128)(2,1)S(1)}, bf16[64,64,256]{2,1,0:T(8,128)(2,1)}, u32[]{:S(2)}) %copy-start) | copy-done | bytes 2097176
  4.1 0.0 copy-start.2
  4.1 1.0 copy-done.2
  5.2 0.0 copy-start.4
  5.2 1.0 copy-done.4
  6.2 0.0 copy-start.6
  6.2 0.8 copy-done.6
  7.0 0.0 copy-start.8
  7.0 0.9 copy-done.8
  7.9 0.0 copy-start.9
  7.9 0.8 copy-done.9
  8.7 0.0 copy-start.10
  8.7 0.8 copy-done.10
  9.5 0.0 copy-start.1
  9.5 0.0 copy-start.3
  9.5 0.0 copy-start.5
  9.5 46.4 %exchange.1 = (bf16[3,3,64,256]{3,2,1,0:T(8,128)(2,1)S(1)}, bf16[3,64,16,256]{3,2,1,0:T(8,128)(2,1)S(1)}, bf16[3,1024,64]{2,1,0:T(8,128)(2,1)S(1)}, bf16[3,128,64]{2,1,0:T(8,128)(2,1)S(1)}, bf16[16,64]{1,0:T(8,128)(2,1)S(1)}) custom-call(bf16[3,64,256]{2,1,0:T(8,128)(2,1)S(1)} %bitcast.26, bf16[64,16,256]{2,1,0:T(8,128)(2,1)S(1)} %copy-done.4, ...), custom_call_target="tpu_custom_call" | custom-call | tf_op jit(solution)/shard_map/exchange/pallas_call | solution.py:430
  55.9 0.0 copy-done.7
  55.9 0.0 copy-done.11
  55.9 0.0 copy-done.1
  55.9 0.0 copy-done.3
  55.9 0.0 copy-done.5
  55.9 92.0 %local.1 = f32[64,16,256]{2,1,0:T(8,128)} custom-call(s32[512]{0:T(512)S(1)} %reshape.30.near_list, s32[64]{0:T(128)S(1)} %copy-done.11, s32[512]{0:T(512)S(1)} %reshape.31.far_leaf, s32[64]{0:T(128)S(1)} %reshape.32.far_cluster, bf16[3,3,64,256]{3,2,1,0:T(8,128)(2,1)S(1)} %get-tuple-element.10.points, ...), custom_call_target="tpu_custom_call" | custom-call | tf_op jit(solution)/shard_map/local/pallas_call | solution.py:456
Async XLA Ops:
  0.0 55.9 %copy-start.7 = (bf16[8,4096]{1,0:T(8,128)(2,1)S(1)}, bf16[8,4096]{1,0:T(8,128)(2,1)}, u32[]{:S(2)}) copy-start(bf16[8,4096]{1,0:T(8,128)(2,1)} %param.21) | copy-start | bytes 196612
  0.0 55.9 %copy-start.11 = (s32[64]{0:T(128)S(1)}, s32[64]{0:T(128)}, u32[]{:S(2)}) copy-start(s32[64]{0:T(128)} %near_count.1) | copy-start | bytes 772
  2.5 1.6 %copy-start = (bf16[64,64,256]{2,1,0:T(8,128)(2,1)S(1)}, bf16[64,64,256]{2,1,0:T(8,128)(2,1)}, u32[]{:S(2)}) copy-start(bf16[64,64,256]{2,1,0:T(8,128)(2,1)} %basis_hbm.1) | copy-start | bytes 6291460
  4.1 1.0 copy-start.2
  5.2 1.0 copy-start.4
  6.2 0.8 copy-start.6
  7.0 0.9 copy-start.8
  7.9 0.8 copy-start.9
  8.7 0.8 copy-start.10
  9.5 46.4 %copy-start.1 = (bf16[64,64,256]{2,1,0:T(8,128)(2,1)S(1)}, bf16[64,64,256]{2,1,0:T(8,128)(2,1)}, u32[]{:S(2)}) copy-start(bf16[64,64,256]{2,1,0:T(8,128)(2,1)} %basis_hbm.1) | copy-start | bytes 6291460
  9.5 46.4 %copy-start.3 = (bf16[64,4096]{1,0:T(8,128)(2,1)S(1)}, bf16[64,4096]{1,0:T(8,128)(2,1)}, u32[]{:S(2)}) copy-start(bf16[64,4096]{1,0:T(8,128)(2,1)} %param.20) | copy-start | bytes 1572868
  9.5 46.4 %copy-start.5 = (bf16[8,8,4096]{2,1,0:T(8,128)(2,1)S(1)}, bf16[8,8,4096]{2,1,0:T(8,128)(2,1)}, u32[]{:S(2)}) copy-start(bf16[8,8,4096]{2,1,0:T(8,128)(2,1)} %param.23) | copy-start | bytes 1572868

commit v2 on v1

v2 whole, which is shorter than its diff:
```python
import functools

import jax
import jax.numpy as jnp
from jax import lax
from jax.experimental import pallas as pl
from jax.experimental.pallas import tpu as pltpu
from jax.sharding import PartitionSpec as P

SOFTENING = 0.0025
ROOT_TWO = 1.4142135623730951
MESH = pl.DeviceIdType.MESH
F32 = jnp.float32
BF16 = jnp.bfloat16
ROWS = 16
EARLY = 2
GROUP = 16


def dot(a, b, left=1, right=0):
    return lax.dot_general(a, b, (((left,), (right,)), ((), ())), preferred_element_type=F32)


def spread_map(parity, rank, links):
    lane = lax.broadcasted_iota(jnp.int32, (rank, rank // 2 * links), 1)
    row = lax.broadcasted_iota(jnp.int32, (rank, rank // 2 * links), 0)
    return jnp.where(row == lane // links * 2 + parity, 1.0, 0.0).astype(BF16)


def link_mask(rows, links, lanes, per_link):
    lane = lax.broadcasted_iota(jnp.int32, (rows, lanes), 1)
    row = lax.broadcasted_iota(jnp.int32, (rows, lanes), 0)
    return jnp.where(lane % links == row // per_link, 1.0, 0.0)


def fold(product, rhs, rank):
    return product[:rhs, :rank] + product[rhs:, rank:]


def gathered_up(stack, maps, mask, links, rhs):
    halves = []
    for spread in maps:
        wide = dot(stack, spread) * mask
        halves.append(wide.reshape(links, rhs, wide.shape[1]).sum(axis=0))
    return jnp.concatenate(halves, axis=0).astype(BF16)


def block_diagonal(value):
    zero = jnp.zeros_like(value)
    upper = jnp.concatenate([value, zero], axis=1)
    lower = jnp.concatenate([zero, value], axis=1)
    return jnp.concatenate([upper, lower], axis=0).astype(BF16)


def spread_down(value, matrix, maps, mask, links, rhs):
    product = dot(block_diagonal(value), matrix, 1, 1)
    total = None
    for parity, spread in enumerate(maps):
        half = product[parity * rhs : (parity + 1) * rhs]
        tall = (jnp.concatenate([half] * links, axis=0) * mask).astype(BF16)
        part = dot(tall, spread, 1, 1)
        total = part if total is None else total + part
    return total


def split(value):
    first = value.astype(BF16).astype(F32)
    second = (value - first).astype(BF16).astype(F32)
    return [first, second, value - first - second]


def augmented(coordinates):
    one = jnp.ones_like(coordinates[0])
    norm = sum(value * value for value in coordinates)
    source = [-512.0 * value for value in coordinates]
    source += [256.0 * value for value in split(norm + SOFTENING)] + [256.0 * one] * 3
    target = coordinates + [one] * 3 + split(norm)
    zero = [jnp.zeros_like(one)] * (ROWS - len(source))
    return source + zero, target + zero


def put_rows(table, rows, at, stride):
    for row, value in enumerate(rows):
        for half in range(value.shape[1] // 128):
            base = (half * ROWS + row) * stride + at
            table[base : base + 16, :] = value[:, half * 128 : half * 128 + 128]


def side_of(table, leaf, stride):
    halves = table.shape[0] // (ROWS * stride)
    pieces = [
        table[pl.ds(half * ROWS * stride + leaf, ROWS, stride=stride), :] for half in range(halves)
    ]
    return jnp.concatenate(pieces, axis=1).astype(BF16)


def near_tile(target_side, source_side):
    return lax.rsqrt(dot(target_side, source_side, 0, 0)).astype(BF16)


def exchange_kernel(
    grid_shape,
    near_list,
    near_count,
    far_leaf,
    far_cluster,
    top_transfer,
    top_coupling,
    points_hbm,
    charges_hbm,
    basis_hbm,
    leaf_maps_hbm,
    parent_maps_hbm,
    parent_couplings_hbm,
    leaf_couplings_hbm,
    wide_points,
    wide_charges,
    partial,
    wide_moments,
    wide_parents,
    own_charges,
    basis,
    leaf_maps,
    parent_maps,
    parent_couplings,
    leaf_couplings,
    target_table,
    source_table,
    target_sides,
    source_sides,
    moment_table,
    parent_table,
    far,
    local,
    sent,
    arrived,
    send_sem,
    recv_sem,
    tree_send,
    tree_recv,
    own_sem,
):
    across, along = grid_shape
    total = across * along
    levels = total.bit_length() - 1
    me = lax.axis_index("gx") * along + lax.axis_index("gy")
    _, leaves, rhs, size = wide_charges.shape
    rank = basis.shape[1]
    parents = leaf_maps.shape[0]
    links = leaves // parents
    slots = near_list.shape[0] // leaves

    def place(index):
        return (index // along, index % along)

    def sibling(height):
        step = 2**height
        return me + step - 2 * step * ((me // step) % 2)

    barrier = pltpu.get_barrier_semaphore()

    @pl.when(me > 0)
    def _():
        pl.semaphore_signal(barrier, inc=1, device_id=place(me - 1), device_id_type=MESH)

    @pl.when(me < total - 1)
    def _():
        pl.semaphore_signal(barrier, inc=1, device_id=place(me + 1), device_id_type=MESH)

    for height in range(levels):
        pl.semaphore_signal(barrier, inc=1, device_id=place(sibling(height)), device_id_type=MESH)

    own = [
        pltpu.make_async_copy(source, target, own_sem.at[index])
        for index, (source, target) in enumerate(
            (
                (points_hbm, wide_points.at[1]),
                (charges_hbm, own_charges),
                (basis_hbm, basis),
                (leaf_maps_hbm, leaf_maps),
                (parent_maps_hbm, parent_maps),
                (parent_couplings_hbm, parent_couplings),
                (leaf_couplings_hbm, leaf_couplings),
                (charges_hbm, wide_charges.at[1]),
            )
        )
    ]
    for copy in own:
        copy.start()
    maps = [spread_map(parity, rank, links) for parity in range(2)]
    lanes = rank // 2 * links
    mask = link_mask(links * rhs, links, lanes, rhs)
    lane = lax.broadcasted_iota(jnp.int32, (2 * rhs, lanes), 1) % links
    masks = [jnp.where(lane == link, 1.0, 0.0).astype(BF16) for link in range(links)]

    arrays = (wide_charges, wide_points, wide_parents, wide_moments)
    mine = (own_charges, wide_points.at[1], wide_parents.at[1], wide_moments.at[1])

    def rightward(index):
        return pltpu.make_async_remote_copy(
            src_ref=mine[index],
            dst_ref=arrays[index].at[0],
            send_sem=send_sem.at[index, 0],
            recv_sem=recv_sem.at[index, 0],
            device_id=place(jnp.minimum(me + 1, total - 1)),
            device_id_type=MESH,
        )

    def leftward(index):
        return pltpu.make_async_remote_copy(
            src_ref=mine[index],
            dst_ref=arrays[index].at[2],
            send_sem=send_sem.at[index, 1],
            recv_sem=recv_sem.at[index, 1],
            device_id=place(jnp.maximum(me - 1, 0)),
            device_id_type=MESH,
        )

    def climb(height):
        return pltpu.make_async_remote_copy(
            src_ref=sent.at[height],
            dst_ref=arrived.at[height],
            send_sem=tree_send.at[height],
            recv_sem=tree_recv.at[height],
            device_id=place(sibling(height)),
            device_id_type=MESH,
        )

    def send(indices):
        @pl.when(me < total - 1)
        def _():
            for index in indices:
                rightward(index).start()

        @pl.when(me > 0)
        def _():
            for index in indices:
                leftward(index).start()

    def settle(indices):
        @pl.when(me < total - 1)
        def _():
            for index in indices:
                rightward(index).wait_send()
                leftward(index).wait_recv()

        @pl.when(me > 0)
        def _():
            for index in indices:
                leftward(index).wait_send()
                rightward(index).wait_recv()

    own[0].wait()
    own[1].wait()
    pl.semaphore_wait(barrier, levels + jnp.where(me > 0, 1, 0) + jnp.where(me < total - 1, 1, 0))
    send((0, 1))
    own[2].wait()
    group = 8

    def one_moment(step, carry):
        for inner in range(group):
            leaf = step * group + inner
            value = dot(own_charges[leaf], basis[leaf], 1, 1).astype(BF16)
            wide_moments[1, pl.ds(pl.multiple_of(leaf * rhs, rhs), rhs), :] = value
        return carry

    lax.fori_loop(0, leaves // group, one_moment, 0)
    own[3].wait()
    for parent in range(parents):
        stack = wide_moments[1, parent * links * rhs : (parent + 1) * links * rhs, :]
        product = dot(gathered_up(stack, maps, mask, links, rhs), leaf_maps[parent])
        wide_parents[1, parent * rhs : (parent + 1) * rhs, :] = fold(product, rhs, rank).astype(BF16)
    own[4].wait()
    product = dot(gathered_up(wide_parents[1], maps, mask, parents, rhs), parent_maps[...])
    sent[0] = fold(product, rhs, rank).astype(BF16)
    climb(0).start()
    send((2, 3))

    @pl.when(me == 0)
    def _():
        wide_moments[0] = jnp.zeros(wide_moments.shape[1:], BF16)
        wide_parents[0] = jnp.zeros(wide_parents.shape[1:], BF16)

    @pl.when(me == total - 1)
    def _():
        wide_moments[2] = jnp.zeros(wide_moments.shape[1:], BF16)
        wide_parents[2] = jnp.zeros(wide_parents.shape[1:], BF16)

    for start in range(0, leaves, 16):
        coordinates = [wide_points[1, axis, start : start + 16, :].astype(F32) for axis in range(3)]
        source_rows, target_rows = augmented(coordinates)
        put_rows(source_table, source_rows, start, leaves)
        put_rows(target_table, target_rows, start, leaves)

    def one_side(step, carry):
        for inner in range(group):
            leaf = step * group + inner
            source_sides[leaf] = side_of(source_table, leaf, leaves)
            target_sides[leaf] = side_of(target_table, leaf, leaves)
        return carry

    lax.fori_loop(0, leaves // group, one_side, 0)
    shift = leaves - me * leaves
    batch = 8

    def own_near(step, carry):
        results = []
        for inner in range(batch):
            leaf = step * batch + inner
            used = near_count[leaf]
            rank_of = 0
            found = [0] * EARLY
            for slot in range(slots):
                source = near_list[leaf * slots + slot] - me * leaves
                inside = (source >= 0) & (source < leaves) & (slot < used)
                for place_at in range(EARLY):
                    found[place_at] = jnp.where(inside & (rank_of == place_at), source, found[place_at])
                rank_of = rank_of + jnp.where(inside, 1, 0)
            tiles = []
            values = []
            for place_at in range(EARLY):
                source = found[place_at]
                tiles.append(near_tile(target_sides[leaf], source_sides[source]))
                weight = jnp.where(rank_of > place_at, 1.0, 0.0).astype(F32)
                values.append((own_charges[source].astype(F32) * weight).astype(BF16))
            wide_tile = jnp.concatenate(tiles, axis=1)
            wide_value = jnp.concatenate(values, axis=1)
            results.append(dot(wide_tile, wide_value, 1, 1).T)
        for inner in range(batch):
            partial[step * batch + inner] = results[inner]
        return carry

    couplings = []
    sides = []
    steps = leaves // batch
    for height in range(levels):
        lax.fori_loop(steps * height // levels, steps * (height + 1) // levels, own_near, 0)
        climb(height).wait()
        side = (me // 2**height) % 2
        sides.append(side)
        other = arrived[height]
        couplings.append(dot(other, top_coupling[side]))
        if height < levels - 1:
            raised = dot(sent[height], top_transfer[side]) + dot(other, top_transfer[1 - side])
            sent[height + 1] = raised.astype(BF16)
            climb(height + 1).start()
    field = couplings[levels - 1]
    for height in reversed(range(levels - 1)):
        field = couplings[height] + ROOT_TWO * dot(field.astype(BF16), top_transfer[sides[height]], 1, 1)
    device_local = field.astype(BF16).astype(F32)

    settle((2, 3))
    for block in range(3):
        for parity in range(2):
            value = dot(wide_moments[block], maps[parity]).astype(BF16)
            moment_table[
                block * leaves : (block + 1) * leaves, parity * rhs : (parity + 1) * rhs, :
            ] = value.reshape(leaves, rhs, value.shape[1])
            value = dot(wide_parents[block], maps[parity]).astype(BF16)
            parent_table[
                block * parents : (block + 1) * parents, parity * rhs : (parity + 1) * rhs, :
            ] = value.reshape(parents, rhs, value.shape[1])

    def collect(table, index, row, offset):
        gathered = None
        for link in range(links):
            at = jnp.clip(index[row * links + link] + offset, 0, table.shape[0] - 1)
            part = table[at] * masks[link]
            gathered = part if gathered is None else gathered + part
        return gathered

    own[5].wait()
    parent_shift = parents - me * parents
    down = spread_down(device_local, parent_maps[...], maps, mask, links, rhs)
    parent_local = []
    for parent in range(parents):
        product = dot(collect(parent_table, far_cluster, parent, parent_shift), parent_couplings[parent])
        value = fold(product, rhs, rank) + down[parent * rhs : (parent + 1) * rhs]
        parent_local.append(value.astype(BF16).astype(F32))
    own[6].wait()

    def some_leaves(step, carry):
        for inner in range(group):
            leaf = step * group + inner
            product = dot(collect(moment_table, far_leaf, leaf, shift), leaf_couplings[leaf])
            far[pl.ds(pl.multiple_of(leaf * rhs, rhs), rhs), :] = fold(product, rhs, rank)
        return carry

    lax.fori_loop(0, leaves // group, some_leaves, 0)
    for parent in range(parents):
        down = spread_down(parent_local[parent], leaf_maps[parent], maps, mask, links, rhs)
        rows = slice(parent * links * rhs, (parent + 1) * links * rhs)
        local[rows, :] = (far[rows, :] + down).astype(BF16)

    def finish(step, carry):
        for inner in range(group):
            leaf = step * group + inner
            value = local[pl.ds(pl.multiple_of(leaf * rhs, rhs), rhs), :]
            partial[leaf] = partial[leaf] + dot(value, basis[leaf])
        return carry

    lax.fori_loop(0, leaves // group, finish, 0)
    own[7].wait()
    settle((0, 1))


def near_kernel(
    grid_shape,
    near_list,
    near_count,
    points,
    charges,
    partial,
    potential,
    target_table,
    source_table,
    pair_source,
    pair_target,
):
    along = grid_shape[1]
    me = lax.axis_index("gx") * along + lax.axis_index("gy")
    _, leaves, rhs, size = charges.shape
    wide = 3 * leaves
    slots = near_list.shape[0] // leaves
    shift = leaves - me * leaves
    group = GROUP

    def list_leaf(leaf, count):
        used = near_count[leaf]
        rank_of = 0
        for slot in range(slots):
            source = near_list[leaf * slots + slot] + shift
            live = slot < used
            inside = (source >= leaves) & (source < 2 * leaves) & live
            done = inside & (rank_of < EARLY)
            pair_source[count] = source
            pair_target[count] = leaf
            count = count + jnp.where(live & jnp.logical_not(done), 1, 0)
            rank_of = rank_of + jnp.where(inside, 1, 0)
        return count

    pairs = lax.fori_loop(0, leaves, list_leaf, 0)
    for extra in range(group):
        pair_source[pairs + extra] = leaves
        pair_target[pairs + extra] = 0

    for block in range(3):
        for start in range(0, leaves, 16):
            coordinates = [points[block, axis, start : start + 16, :].astype(F32) for axis in range(3)]
            source_rows, target_rows = augmented(coordinates)
            put_rows(source_table, source_rows, block * leaves + start, wide)
            if block == 1:
                put_rows(target_table, target_rows, start, leaves)
    potential[...] = partial[...]

    def some_pairs(step, carry):
        results = []
        for inner in range(group):
            at = step * group + inner
            source = pair_source[at]
            target = pair_target[at]
            tile = near_tile(side_of(target_table, target, leaves), side_of(source_table, source, wide))
            value = dot(tile, charges[source // leaves, source % leaves], 1, 1).T
            results.append((target, jnp.where(at < pairs, value, 0.0)))
        for target, value in results:
            potential[target] = potential[target] + value
        return carry

    lax.fori_loop(0, (pairs + group - 1) // group, some_pairs, 0)


def stored(matrix, links):
    length = matrix.shape[-1]
    tiles = length // 128
    value = matrix.reshape(-1, links, tiles, 128).transpose(0, 2, 1, 3)
    return value.reshape(-1, tiles * links, 128)


def on_device(
    grid_shape,
    points,
    charges,
    near_list,
    near_count,
    far_leaf,
    far_cluster,
    basis,
    leaf_transfer,
    cluster_transfer,
    leaf_coupling,
    cluster_coupling,
    top_transfer,
    top_coupling,
):
    leaves, rhs, size = charges.shape
    rank = basis.shape[1]
    parents = cluster_transfer.shape[0]
    links = far_leaf.shape[1]
    levels = (grid_shape[0] * grid_shape[1]).bit_length() - 1
    turned = points.transpose(1, 0, 2)
    leaf_maps = stored(leaf_transfer, links)
    parent_maps = stored(cluster_transfer, links)[0]
    leaf_couplings = stored(leaf_coupling, links)
    parent_couplings = stored(cluster_coupling, links)
    vmem = pl.BlockSpec(memory_space=pltpu.VMEM)
    smem = pl.BlockSpec(memory_space=pltpu.SMEM)
    hbm = pl.BlockSpec(memory_space=pl.ANY)
    shape = jax.ShapeDtypeStruct
    near_flat = near_list.reshape(-1)
    slots = near_list.shape[1]
    spread = rank // 2 * links
    halves = size // 128
    wide_points, wide_charges, partial = pl.pallas_call(
        functools.partial(exchange_kernel, grid_shape),
        out_shape=(
            shape((3,) + turned.shape, BF16),
            shape((3,) + charges.shape, BF16),
            shape((leaves, rhs, size), F32),
        ),
        in_specs=[smem] * 4 + [vmem] * 2 + [hbm] * 7,
        out_specs=(vmem, vmem, vmem),
        scratch_shapes=[
            pltpu.VMEM((3, leaves * rhs, rank), BF16),
            pltpu.VMEM((3, parents * rhs, rank), BF16),
            pltpu.VMEM(charges.shape, BF16),
            pltpu.VMEM(basis.shape, BF16),
            pltpu.VMEM(leaf_maps.shape, BF16),
            pltpu.VMEM(parent_maps.shape, BF16),
            pltpu.VMEM(parent_couplings.shape, BF16),
            pltpu.VMEM(leaf_couplings.shape, BF16),
            pltpu.VMEM((halves * ROWS * leaves, 128), F32),
            pltpu.VMEM((halves * ROWS * leaves, 128), F32),
            pltpu.VMEM((leaves, ROWS, size), BF16),
            pltpu.VMEM((leaves, ROWS, size), BF16),
            pltpu.VMEM((3 * leaves, 2 * rhs, spread), BF16),
            pltpu.VMEM((3 * parents, 2 * rhs, spread), BF16),
            pltpu.VMEM((leaves * rhs, rank), F32),
            pltpu.VMEM((leaves * rhs, rank), BF16),
            pltpu.VMEM((levels, rhs, rank), BF16),
            pltpu.VMEM((levels, rhs, rank), BF16),
            pltpu.SemaphoreType.DMA((4, 2)),
            pltpu.SemaphoreType.DMA((4, 2)),
            pltpu.SemaphoreType.DMA((levels,)),
            pltpu.SemaphoreType.DMA((levels,)),
            pltpu.SemaphoreType.DMA((8,)),
        ],
        compiler_params=pltpu.CompilerParams(
            collective_id=0, has_side_effects=True, vmem_limit_bytes=48 << 20
        ),
        name="exchange",
    )(
        near_flat,
        near_count,
        far_leaf.reshape(-1),
        far_cluster.reshape(-1),
        top_transfer,
        top_coupling,
        turned,
        charges,
        basis,
        leaf_maps,
        parent_maps,
        parent_couplings,
        leaf_couplings,
    )
    return pl.pallas_call(
        functools.partial(near_kernel, grid_shape),
        out_shape=shape((leaves, rhs, size), F32),
        in_specs=[smem] * 2 + [vmem] * 3,
        out_specs=vmem,
        scratch_shapes=[
            pltpu.VMEM((halves * ROWS * leaves, 128), F32),
            pltpu.VMEM((halves * ROWS * 3 * leaves, 128), F32),
            pltpu.SMEM((leaves * slots + GROUP,), jnp.int32),
            pltpu.SMEM((leaves * slots + GROUP,), jnp.int32),
        ],
        compiler_params=pltpu.CompilerParams(vmem_limit_bytes=40 << 20),
        name="near",
    )(near_flat, near_count, wide_points, wide_charges, partial)


def solution(mesh):
    grid_shape = (mesh.shape["gx"], mesh.shape["gy"])
    both = ("gx", "gy")
    in_specs = (
        P(both, None, None),
        P(both, None, None),
        P(both, None),
        P(both),
        P(both, None),
        P(both, None),
        P(both, None, None),
        P(both, None),
        P(both, None),
        P(both, None, None),
        P(both, None, None),
        P(),
        P(),
    )
    return jax.shard_map(
        functools.partial(on_device, grid_shape),
        mesh=mesh,
        in_specs=in_specs,
        out_specs=P(both, None, None),
        check_vma=False,
    )
```

time: 148 us -> 96.5 us (0.65)
  the two profiles are of different devices: /device:TPU:25 before, /device:TPU:2 now
where the time goes in v2:
time: 96.5 us; the launch traced here: 96.8 us
  Pallas kernels  87.3 us (90%)
  local copies, waits for them, and re-layouts  9.51 us (10%)
    pallas_call x1, Pallas kernels, on_device(): pl.pallas_call(functools.partial(exchange_kernel, grid_shape), out_shape=...  60.2 us
    pallas_call x1, Pallas kernels, on_device(): pl.pallas_call(functools.partial(near_kernel, grid_shape), out_shape=shap...  27 us
    unnamed x18, local copies, waits for them, and re-layouts  8.56 us

profile of v2, /device:TPU:2, one launch (start us, length us, event | category | flops | bytes accessed | tf_op | source)
XLA Modules:
  0.0 96.8 jit_solution(13070756103388467077)
XLA Ops:
  0.0 0.8 reshape.32.far_cluster
  0.8 0.8 copy.14
  1.5 0.1 reshape.30.near_list
  1.6 0.8 copy.15
  2.4 0.1 reshape.31.far_leaf
  2.5 0.0 copy-start
  2.5 1.0 %copy-done = bf16[64,16,256]{2,1,0:T(8,128)(2,1)S(1)} copy-done((bf16[64,16,256]{2,1,0:T(8,128)(2,1)S(1)}, bf16[64,16,256]{2,1,0:T(8,128)(2,1)}, u32[]{:S(2)}) %copy-start) | copy-done | bytes 524312
  3.5 0.0 copy-start.1
  3.5 1.0 %copy-done.1 = bf16[64,4096]{1,0:T(8,128)(2,1)S(1)} copy-done((bf16[64,4096]{1,0:T(8,128)(2,1)S(1)}, bf16[64,4096]{1,0:T(8,128)(2,1)}, u32[]{:S(2)}) %copy-start.1) | copy-done | bytes 524312
  4.6 0.0 copy-start.2
  4.6 1.0 %copy-done.2 = bf16[8,8,4096]{2,1,0:T(8,128)(2,1)S(1)} copy-done((bf16[8,8,4096]{2,1,0:T(8,128)(2,1)S(1)}, bf16[8,8,4096]{2,1,0:T(8,128)(2,1)}, u32[]{:S(2)}) %copy-start.2) | copy-done | bytes 524312
  5.6 0.0 copy-start.3
  5.6 0.9 copy-done.3
  6.5 0.0 copy-start.4
  6.5 0.8 copy-done.4
  7.4 0.0 copy-start.5
  7.4 0.8 copy-done.5
  8.1 0.0 copy-start.6
  8.1 0.8 copy-done.6
  8.9 0.0 copy-start.7
  8.9 0.7 copy-done.7
  9.5 60.2 %exchange.1 = (bf16[3,3,64,256]{3,2,1,0:T(8,128)(2,1)S(1)}, bf16[3,64,16,256]{3,2,1,0:T(8,128)(2,1)S(1)}, f32[64,16,256]{2,1,0:T(8,128)S(1)}) custom-call(s32[512]{0:T(512)S(1)} %reshape.30.near_list, s32[64]{0:T(128)S(1)} %copy-done.7, s32[512]{0:T(512)S(1)} %reshape.31.far_leaf, s32[64]{0:T(128)S(1)} %reshape.32.far_cluster, ...), custom_call_target="tpu_custom_call" | custom-call | tf_op jit(solution)/shard_map/exchange/pallas_call | solution.py:513
  69.8 27.0 %near.1 = f32[64,16,256]{2,1,0:T(8,128)} custom-call(s32[512]{0:T(512)S(1)} %reshape.30.near_list, s32[64]{0:T(128)S(1)} %copy-done.7, bf16[3,3,64,256]{3,2,1,0:T(8,128)(2,1)S(1)} %get-tuple-element.8.points, bf16[3,64,16,256]{3,2,1,0:T(8,128)(2,1)S(1)} %get-tuple-element.9.charges, f32[64,16,256]{2,1,0:T(8,128)S(1)} %get-tuple-element.10.partial), custom_call_target="tpu_custom_call" | custom-call | tf_op jit(solution)/shard_map/near/pallas_call | solution.py:566
Async XLA Ops:
  2.5 1.0 %copy-start = (bf16[64,16,256]{2,1,0:T(8,128)(2,1)S(1)}, bf16[64,16,256]{2,1,0:T(8,128)(2,1)}, u32[]{:S(2)}) copy-start(bf16[64,16,256]{2,1,0:T(8,128)(2,1)} %charges_hbm.1) | copy-start | bytes 1572868
  3.5 1.0 %copy-start.1 = (bf16[64,4096]{1,0:T(8,128)(2,1)S(1)}, bf16[64,4096]{1,0:T(8,128)(2,1)}, u32[]{:S(2)}) copy-start(bf16[64,4096]{1,0:T(8,128)(2,1)} %param.20) | copy-start | bytes 1572868
  4.6 1.0 %copy-start.2 = (bf16[8,8,4096]{2,1,0:T(8,128)(2,1)S(1)}, bf16[8,8,4096]{2,1,0:T(8,128)(2,1)}, u32[]{:S(2)}) copy-start(bf16[8,8,4096]{2,1,0:T(8,128)(2,1)} %param.23) | copy-start | bytes 1572868
  5.6 0.9 copy-start.3
  6.5 0.8 copy-start.4
  7.4 0.8 copy-start.5
  8.1 0.8 copy-start.6
  8.9 0.7 copy-start.7

commit v3 on v2

--- a/solution.py
+++ b/solution.py
@@ -253,7 +253,6 @@
     own[0].wait()
     own[1].wait()
     pl.semaphore_wait(barrier, levels + jnp.where(me > 0, 1, 0) + jnp.where(me < total - 1, 1, 0))
-    send((0, 1))
     own[2].wait()
     group = 8
 
@@ -275,6 +274,7 @@
     sent[0] = fold(product, rhs, rank).astype(BF16)
     climb(0).start()
     send((2, 3))
+    send((0, 1))
 
     @pl.when(me == 0)
     def _():
@@ -330,11 +330,45 @@
             partial[step * batch + inner] = results[inner]
         return carry
 
+    def collect(table, index, row, offset):
+        gathered = None
+        for link in range(links):
+            at = jnp.clip(index[row * links + link] + offset, 0, table.shape[0] - 1)
+            part = table[at] * masks[link]
+            gathered = part if gathered is None else gathered + part
+        return gathered
+
+    def far_leaves():
+        settle((2, 3))
+        for block in range(3):
+            for parity in range(2):
+                value = dot(wide_moments[block], maps[parity]).astype(BF16)
+                moment_table[
+                    block * leaves : (block + 1) * leaves, parity * rhs : (parity + 1) * rhs, :
+                ] = value.reshape(leaves, rhs, value.shape[1])
+                value = dot(wide_parents[block], maps[parity]).astype(BF16)
+                parent_table[
+                    block * parents : (block + 1) * parents, parity * rhs : (parity + 1) * rhs, :
+                ] = value.reshape(parents, rhs, value.shape[1])
+
+        own[6].wait()
+
+        def some_leaves(step, carry):
+            for inner in range(group):
+                leaf = step * group + inner
+                product = dot(collect(moment_table, far_leaf, leaf, shift), leaf_couplings[leaf])
+                far[pl.ds(pl.multiple_of(leaf * rhs, rhs), rhs), :] = fold(product, rhs, rank)
+            return carry
+
+        lax.fori_loop(0, leaves // group, some_leaves, 0)
+
     couplings = []
     sides = []
     steps = leaves // batch
     for height in range(levels):
         lax.fori_loop(steps * height // levels, steps * (height + 1) // levels, own_near, 0)
+        if height == levels // 2:
+            far_leaves()
         climb(height).wait()
         side = (me // 2**height) % 2
         sides.append(side)
@@ -349,26 +383,6 @@
         field = couplings[height] + ROOT_TWO * dot(field.astype(BF16), top_transfer[sides[height]], 1, 1)
     device_local = field.astype(BF16).astype(F32)
 
-    settle((2, 3))
-    for block in range(3):
-        for parity in range(2):
-            value = dot(wide_moments[block], maps[parity]).astype(BF16)
-            moment_table[
-                block * leaves : (block + 1) * leaves, parity * rhs : (parity + 1) * rhs, :
-            ] = value.reshape(leaves, rhs, value.shape[1])
-            value = dot(wide_parents[block], maps[parity]).astype(BF16)
-            parent_table[
-                block * parents : (block + 1) * parents, parity * rhs : (parity + 1) * rhs, :
-            ] = value.reshape(parents, rhs, value.shape[1])
-
-    def collect(table, index, row, offset):
-        gathered = None
-        for link in range(links):
-            at = jnp.clip(index[row * links + link] + offset, 0, table.shape[0] - 1)
-            part = table[at] * masks[link]
-            gathered = part if gathered is None else gathered + part
-        return gathered
-
     own[5].wait()
     parent_shift = parents - me * parents
     down = spread_down(device_local, parent_maps[...], maps, mask, links, rhs)
@@ -377,16 +391,6 @@
         product = dot(collect(parent_table, far_cluster, parent, parent_shift), parent_couplings[parent])
         value = fold(product, rhs, rank) + down[parent * rhs : (parent + 1) * rhs]
         parent_local.append(value.astype(BF16).astype(F32))
-    own[6].wait()
-
-    def some_leaves(step, carry):
-        for inner in range(group):
-            leaf = step * group + inner
-            product = dot(collect(moment_table, far_leaf, leaf, shift), leaf_couplings[leaf])
-            far[pl.ds(pl.multiple_of(leaf * rhs, rhs), rhs), :] = fold(product, rhs, rank)
-        return carry
-
-    lax.fori_loop(0, leaves // group, some_leaves, 0)
     for parent in range(parents):
         down = spread_down(parent_local[parent], leaf_maps[parent], maps, mask, links, rhs)
         rows = slice(parent * links * rhs, (parent + 1) * links * rhs)

time: 96.5 us -> 85.9 us (0.89); the launches traced: 96.8 us -> 85.1 us
  Pallas kernels: 87.3 us -> 75.6 us
    pallas_call x1, Pallas kernels: 60.2 us -> 50.1 us  [on_device(): pl.pallas_call(functools.partial(exchange_kernel, grid_shape), out_shape=...]
    pallas_call x1, Pallas kernels: 27 us -> 25.5 us  [on_device(): pl.pallas_call(functools.partial(near_kernel, grid_shape), out_shape=shap...]
where the time goes in v3:
time: 85.9 us; the launch traced here: 85.1 us
  Pallas kernels  75.6 us (88%)
  local copies, waits for them, and re-layouts  9.51 us (11%)
    pallas_call x1, Pallas kernels, on_device(): pl.pallas_call(functools.partial(exchange_kernel, grid_shape), out_shape=...  50.1 us
    pallas_call x1, Pallas kernels, on_device(): pl.pallas_call(functools.partial(near_kernel, grid_shape), out_shape=shap...  25.5 us
    unnamed x18, local copies, waits for them, and re-layouts  8.56 us

profile of v3, /device:TPU:2, one launch (start us, length us, event | category | flops | bytes accessed | tf_op | source)
XLA Modules:
  0.0 85.1 jit_solution(9300541083265047186)
XLA Ops:
  0.0 0.8 reshape.32.far_cluster
  0.8 0.8 copy.14
  1.5 0.1 reshape.30.near_list
  1.6 0.8 copy.15
  2.4 0.1 reshape.31.far_leaf
  2.5 0.0 copy-start
  2.5 1.0 %copy-done = bf16[64,16,256]{2,1,0:T(8,128)(2,1)S(1)} copy-done((bf16[64,16,256]{2,1,0:T(8,128)(2,1)S(1)}, bf16[64,16,256]{2,1,0:T(8,128)(2,1)}, u32[]{:S(2)}) %copy-start) | copy-done | bytes 524312
  3.5 0.0 copy-start.1
  3.5 1.0 %copy-done.1 = bf16[64,4096]{1,0:T(8,128)(2,1)S(1)} copy-done((bf16[64,4096]{1,0:T(8,128)(2,1)S(1)}, bf16[64,4096]{1,0:T(8,128)(2,1)}, u32[]{:S(2)}) %copy-start.1) | copy-done | bytes 524312
  4.6 0.0 copy-start.2
  4.6 1.0 %copy-done.2 = bf16[8,8,4096]{2,1,0:T(8,128)(2,1)S(1)} copy-done((bf16[8,8,4096]{2,1,0:T(8,128)(2,1)S(1)}, bf16[8,8,4096]{2,1,0:T(8,128)(2,1)}, u32[]{:S(2)}) %copy-start.2) | copy-done | bytes 524312
  5.6 0.0 copy-start.3
  5.6 0.9 %copy-done.3 = bf16[64,3,256]{2,0,1:T(8,128)(2,1)S(1)} copy-done((bf16[64,3,256]{2,0,1:T(8,128)(2,1)S(1)}, bf16[64,3,256]{2,0,1:T(8,128)(2,1)}, u32[]{:S(2)}) %copy-start.3) | copy-done | bytes 98328
  6.5 0.0 copy-start.4
  6.5 0.8 copy-done.4
  7.4 0.0 copy-start.5
  7.4 0.8 copy-done.5
  8.1 0.0 copy-start.6
  8.1 0.8 copy-done.6
  8.9 0.0 copy-start.7
  8.9 0.7 copy-done.7
  9.5 50.1 %exchange.1 = (bf16[3,3,64,256]{3,2,1,0:T(8,128)(2,1)S(1)}, bf16[3,64,16,256]{3,2,1,0:T(8,128)(2,1)S(1)}, f32[64,16,256]{2,1,0:T(8,128)S(1)}) custom-call(s32[512]{0:T(512)S(1)} %reshape.30.near_list, s32[64]{0:T(128)S(1)} %copy-done.7, s32[512]{0:T(512)S(1)} %reshape.31.far_leaf, s32[64]{0:T(128)S(1)} %reshape.32.far_cluster, ...), custom_call_target="tpu_custom_call" | custom-call | tf_op jit(solution)/shard_map/exchange/pallas_call | solution.py:517
  59.7 25.5 %near.1 = f32[64,16,256]{2,1,0:T(8,128)} custom-call(s32[512]{0:T(512)S(1)} %reshape.30.near_list, s32[64]{0:T(128)S(1)} %copy-done.7, bf16[3,3,64,256]{3,2,1,0:T(8,128)(2,1)S(1)} %get-tuple-element.8.points, bf16[3,64,16,256]{3,2,1,0:T(8,128)(2,1)S(1)} %get-tuple-element.9.charges, f32[64,16,256]{2,1,0:T(8,128)S(1)} %get-tuple-element.10.partial), custom_call_target="tpu_custom_call" | custom-call | tf_op jit(solution)/shard_map/near/pallas_call | solution.py:570
Async XLA Ops:
  2.5 1.0 %copy-start = (bf16[64,16,256]{2,1,0:T(8,128)(2,1)S(1)}, bf16[64,16,256]{2,1,0:T(8,128)(2,1)}, u32[]{:S(2)}) copy-start(bf16[64,16,256]{2,1,0:T(8,128)(2,1)} %charges_hbm.1) | copy-start | bytes 1572868
  3.5 1.0 %copy-start.1 = (bf16[64,4096]{1,0:T(8,128)(2,1)S(1)}, bf16[64,4096]{1,0:T(8,128)(2,1)}, u32[]{:S(2)}) copy-start(bf16[64,4096]{1,0:T(8,128)(2,1)} %param.20) | copy-start | bytes 1572868
  4.6 1.0 %copy-start.2 = (bf16[8,8,4096]{2,1,0:T(8,128)(2,1)S(1)}, bf16[8,8,4096]{2,1,0:T(8,128)(2,1)}, u32[]{:S(2)}) copy-start(bf16[8,8,4096]{2,1,0:T(8,128)(2,1)} %param.23) | copy-start | bytes 1572868
  5.6 0.9 %copy-start.3 = (bf16[64,3,256]{2,0,1:T(8,128)(2,1)S(1)}, bf16[64,3,256]{2,0,1:T(8,128)(2,1)}, u32[]{:S(2)}) copy-start(bf16[64,3,256]{2,0,1:T(8,128)(2,1)} %param.13) | copy-start | bytes 294916
  6.5 0.8 copy-start.4
  7.4 0.8 copy-start.5
  8.1 0.8 copy-start.6
  8.9 0.7 copy-start.7
